TPU v7x, 256 devices: a whole 4x4x8 slice. The times are simulated.
256 devices in a mesh: row: 32 (over z, y), col: 8 (over x, core).
Axes of the slice: x: 4, y: 4, z: 8, core: 2. Of those that a mesh axis runs over, the one named last changes fastest.
Arguments:
- feats: bfloat16 [131072, 256], P(('row', 'col')), may hold values from -6 to 6
- w_msg: bfloat16 [256, 256], replicated, may hold values from -0.375 to 0.375
- w_self: bfloat16 [256, 256], replicated, may hold values from -0.375 to 0.375
- bias: float32 [256], replicated, may hold values from -3 to 3
- hit_mask: int32 [131072], P(('row', 'col')), may hold values 0 or 1
- block_cols: int32 [32, 8, 96], P('row', 'col'), may hold values from 0 to 127, as said below
- block_count: int32 [32, 8], P('row', 'col'), may hold values from 32 to 96, as said below
- edge_vals: bfloat16 [32, 8, 96, 128, 128], P('row', 'col'), may hold values from -0.125 to 0.125
- grad_out: bfloat16 [131072, 256], P(('row', 'col')), may hold values from -3 to 3
Outputs:
- hidden: bfloat16 [131072, 256], P(('row', 'col'))
- grad_feats: bfloat16 [131072, 256], P(('row', 'col'))
- edge_grad: bfloat16 [32, 8, 96, 128, 128], P('row', 'col')
- w_msg_grad: float32 [256, 256], replicated
- w_self_grad: float32 [256, 256], replicated
- bias_grad: float32 [256], replicated
Inputs may be any that keep to these rules, and one draw needn't show every extreme that they name: `block_cols`: slot s of a tile serves the tile's local block row s % 32; the block columns of the slots that serve one block row of one tile are different. Slots from block_count on are unused.
All inputs are finite; a program needn't handle non-finite values. No bound on the sum of `hit_mask` on one device may be relied on, other than what follows from the above.
Results may differ from a plain program's by a relative error of at most 0.015.
Values may be sent and summed in bfloat16 or wider, within the bound.
A program may use at most 128 MiB of HBM per device.

v0:
```python
import math
import jax
import jax.numpy as jnp
from jax import lax
from jax.sharding import PartitionSpec as P


def activate(pre, row_mask, grad_in):
    sig = jax.nn.sigmoid(pre)
    hidden = (pre * sig * row_mask).astype(jnp.bfloat16)
    deriv = sig * (1.0 + pre * (1.0 - sig))
    grad_pre = (grad_in.astype(jnp.float32) * row_mask * deriv).astype(jnp.bfloat16)
    return (hidden, grad_pre)


def per_device(feats, w_msg, w_self, bias, hit_mask, block_cols, block_count, edge_vals, grad_out):
    row_count = lax.axis_size("row")
    col_count = lax.axis_size("col")
    own_rows = feats.shape[0]
    width = feats.shape[1]
    row_mask = hit_mask.astype(jnp.float32)[:, None]
    messages = (jnp.dot(feats, w_msg, preferred_element_type=jnp.float32) * row_mask).astype(
        jnp.bfloat16
    )
    column_msgs = lax.all_gather(messages, "row", axis=0, tiled=True)
    slot_cols = block_cols[0, 0]
    edge_block = edge_vals[0, 0]
    slot_total = edge_block.shape[0]
    edge_size = edge_block.shape[1]
    tile_rows = col_count * own_rows // edge_size
    tile_cols = row_count * own_rows // edge_size
    slot_depth = slot_total // tile_rows
    slot_flags = jnp.arange(slot_total, dtype=jnp.int32) < block_count[0, 0]
    edge_live = (edge_block * slot_flags.astype(jnp.bfloat16)[:, None, None]).reshape(
        slot_depth, tile_rows, edge_size, edge_size
    )
    col_blocks = column_msgs.reshape(tile_cols, edge_size, width)[slot_cols].reshape(
        slot_depth, tile_rows, edge_size, width
    )
    partial_value = jnp.einsum(
        "krij,krjf->rif", edge_live, col_blocks, preferred_element_type=jnp.float32
    ).reshape(tile_rows * edge_size, width)
    summed = lax.psum_scatter(
        partial_value.astype(jnp.bfloat16), "col", scatter_dimension=0, tiled=True
    ).astype(jnp.float32)
    pre = summed + jnp.dot(feats, w_self, preferred_element_type=jnp.float32) + bias
    hidden, grad_pre = activate(pre, row_mask, grad_out)
    grad_rows_all = lax.all_gather(grad_pre, "col", axis=0, tiled=True)
    grad_tile = grad_rows_all.reshape(tile_rows, edge_size, width)
    backward = jnp.einsum(
        "krij,rif->krjf", edge_live, grad_tile, preferred_element_type=jnp.float32
    ).reshape(slot_total, edge_size, width)
    back_part = jax.ops.segment_sum(backward, slot_cols, num_segments=tile_cols).reshape(
        tile_cols * edge_size, width
    )
    edge_grad = (
        jnp.einsum(
            "rif,krjf->krij", grad_tile, col_blocks, preferred_element_type=jnp.float32
        ).reshape(slot_total, edge_size, edge_size)
        * slot_flags.astype(jnp.float32)[:, None, None]
    ).astype(jnp.bfloat16)
    grad_sum = lax.psum_scatter(
        back_part.astype(jnp.bfloat16), "row", scatter_dimension=0, tiled=True
    ).astype(jnp.float32)
    grad_msg = (grad_sum * row_mask).astype(jnp.bfloat16)
    grad_feats = (
        jnp.einsum("hg,fg->hf", grad_msg, w_msg, preferred_element_type=jnp.float32)
        + jnp.einsum("hg,fg->hf", grad_pre, w_self, preferred_element_type=jnp.float32)
    ).astype(jnp.bfloat16)
    local_msg = jnp.einsum("hf,hg->fg", feats, grad_msg, preferred_element_type=jnp.float32)
    local_self = jnp.einsum("hf,hg->fg", feats, grad_pre, preferred_element_type=jnp.float32)
    local_bias = jnp.sum(grad_pre.astype(jnp.float32), axis=0)
    total_msg, total_self, total_bias = lax.psum(
        (local_msg, local_self, local_bias), ("row", "col")
    )
    factor = 1.0 / math.sqrt(own_rows * row_count * col_count)
    return (
        hidden,
        grad_feats,
        edge_grad[None, None],
        total_msg * factor,
        total_self * factor,
        total_bias * factor,
    )


def solution(mesh):
    placed = (
        P(("row", "col"), None),
        P(),
        P(),
        P(),
        P(("row", "col")),
        P("row", "col", None),
        P("row", "col"),
        P("row", "col", None, None, None),
        P(("row", "col"), None),
    )
    return jax.shard_map(
        per_device,
        mesh=mesh,
        in_specs=placed,
        out_specs=(
            P(("row", "col"), None),
            P(("row", "col"), None),
            P("row", "col", None, None, None),
            P(),
            P(),
            P(),
        ),
        check_vma=False,
    )
```

profile of v0, /device:TPU:2, one launch (start us, length us, event | category | flops | bytes accessed | tf_op | source)
XLA Modules:
  0.0 757.9 jit_solution(17679265204071514697)
XLA Ops:
  7.2 0.0 copy-start
  7.2 0.0 all-gather.3.cloned.1.call-start
  7.2 0.7 convert_element_type.67
  7.9 0.2 copy-done
  8.1 1.8 fusion.12
  10.0 0.0 all-gather.3.cloned.1.call-update
  10.0 0.0 reduce-scatter.3.cloned.1.call-start
  10.7 0.7 fusion.16
  11.4 100.7 %all-gather.3.cloned.1.call-done = bf16[16384,256]{1,0:T(8,128)(2,1)} async-done(((bf16[512,256]{1,0:T(8,128)(2,1)}), bf16[16384,256]{1,0:T(8,128)(2,1)}) %all-gather.3.cloned.1.call-update) | async-done | bytes 8388624 | tf_op jit(solution)/shard_map/all_gather | solution.py:25
  112.0 0.0 copy-start.2
  112.0 9.5 %gather_fusion = bf16[96,128,256]{2,1,0:T(8,128)(2,1)} fusion(bf16[128,128,256]{2,1,0:T(8,128)(2,1)} %bitcast.53, s32[1024]{0:T(1024)S(1)} %pad_clamp_fusion), kind=kCustom, calls=%fused_computation | custom fusion | bytes 12583296 | tf_op jit(solution)/shard_map/gather | solution.py:37
  121.5 0.0 copy-done.2
  121.5 0.0 copy-start.5
  121.5 5.5 bitcast_convert_fusion
  127.0 0.0 reduce-scatter.3.cloned.1.call-update
  127.0 0.0 all-gather.5.cloned.1.call-start
  127.1 30.4 %reduce-scatter.3.cloned.1.call-done = bf16[512,256]{1,0:T(8,128)(2,1)} async-done(((bf16[4096,256]{1,0:T(8,128)(2,1)}), bf16[512,256]{1,0:T(8,128)(2,1)}) %reduce-scatter.3.cloned.1.call-update) | async-done | bytes 262160 | tf_op jit(solution)/shard_map/reduce_scatter | solution.py:43
  157.5 0.0 copy-done.5
  157.5 2.3 convert_reduce_fusion
  159.8 0.0 all-gather.5.cloned.1.call-update
  159.8 0.0 reduce-scatter.5.cloned.1.call-start
  159.9 28.7 %all-gather.5.cloned.1.call-done = bf16[4096,256]{1,0:T(8,128)(2,1)} async-done(((bf16[512,256]{1,0:T(8,128)(2,1)}), bf16[4096,256]{1,0:T(8,128)(2,1)}) %all-gather.5.cloned.1.call-update) | async-done | bytes 2097168 | tf_op jit(solution)/shard_map/all_gather | solution.py:48
  188.6 8.0 %convolution_bitcast_fusion = f32[3,32,128,256]{2,3,0,1:T(8,128)} fusion(bf16[32,128,256,1]{2,1,3,0:T(8,128)(2,1)} %bitcast.51, bf16[3,32,128,128]{3,2,1,0:T(8,128)(2,1)S(1)} %bitcast.55, bf16[3,32]{0,1:T(8,128)(2,1)S(1)} %fusion.15), kind=kOutput, calls=%fused_computation.7 | convolution fusion | flops 811597824 | bytes 17825984 | tf_op jit(solution)/shard_map/krij,rif->krjf/dot_general | solution.py:50
  196.6 12.6 %copy.22 = f32[3,32,128,256]{3,2,1,0:T(8,128)} copy(f32[3,32,128,256]{2,3,0,1:T(8,128)} %convolution_bitcast_fusion) | data formatting | bytes 25165824 | tf_op jit(solution)/shard_map/krij,rif->krjf/transpose | solution.py:50
  209.2 7.8 %broadcast_in_dim.2 = f32[128,128,256]{2,1,0:T(8,128)} broadcast(f32[]{:T(128)} %constant.4.clone.1), dimensions={} | broadcast | bytes 16777220 | tf_op jit(solution)/shard_map/broadcast_in_dim | solution.py:53
  217.0 0.0 copy-done.6
  217.0 29.1 %scatter_fusion = f32[128,128,256]{2,1,0:T(8,128)} fusion(f32[128,128,256]{2,1,0:T(8,128)} %broadcast_in_dim.2, s32[96]{0:T(128)S(1)} %bitcast.57, f32[96,128,256]{2,1,0:T(8,128)} %bitcast.46), kind=kCustom, calls=%fused_computation.1 | custom fusion | flops 3145728 | bytes 37749120 | tf_op jit(solution)/shard_map/scatter-add | solution.py:53
  246.1 9.0 %convert_element_type.75 = bf16[128,128,256]{2,1,0:T(8,128)(2,1)} convert(f32[128,128,256]{2,1,0:T(8,128)} %scatter_fusion) | non-fusion elementwise | flops 4194304 | bytes 25165824 | tf_op jit(solution)/shard_map/convert_element_type | solution.py:63
  255.1 0.0 reduce-scatter.5.cloned.1.call-update
  255.2 0.0 all-reduce.3.cloned.1.call-start
  255.2 78.1 %psum.23 = f32[256]{0:T(256)S(1)} all-reduce(f32[256]{0:T(256)S(1)} %get-tuple-element.20), channel_id=1, replica_groups=mesh['row'=32,'col'=8] {'row','col'}, use_global_device_ids=true, to_apply=%region_6.0 | all-reduce | flops 256 | bytes 2048 | tf_op jit(solution)/shard_map/psum | solution.py:73
  333.3 0.6 broadcast_multiply_fusion.2
  333.9 0.0 copy-done.3
  333.9 1.0 convolution_bitcast_fusion.1
  334.9 0.0 copy-done.1
  334.9 7.3 fusion.4
  342.1 6.6 copy.24
  348.7 5.1 multiply_convert_fusion
  353.8 134.4 %reduce-scatter.5.cloned.1.call-done = bf16[512,256]{1,0:T(8,128)(2,1)} async-done(((bf16[16384,256]{1,0:T(8,128)(2,1)}), bf16[512,256]{1,0:T(8,128)(2,1)}) %reduce-scatter.5.cloned.1.call-update) | async-done | bytes 262160 | tf_op jit(solution)/shard_map/reduce_scatter | solution.py:62
  488.2 2.0 convolution_bitcast_fusion.2
  490.2 0.0 all-reduce.3.cloned.1.call-update
  490.2 0.0 copy-done.4
  490.2 1.2 fusion.14
  491.4 1.0 fusion.13
  492.4 256.2 %all-reduce.3.cloned.1.call-done = (f32[256,256]{0,1:T(8,128)}, f32[256,256]{0,1:T(8,128)}) async-done(((f32[256,256]{0,1:T(8,128)}, f32[256,256]{0,1:T(8,128)}), (f32[256,256]{0,1:T(8,128)}, f32[256,256]{0,1:T(8,128)})) %all-reduce.3.cloned.1.call-update) | async-done | bytes 524304 | tf_op jit(solution)/shard_map/psum | solution.py:73
  748.6 1.1 broadcast_multiply_fusion
  749.7 0.8 copy.26
  750.5 0.8 copy.25
  (7 shorter events, 0.0 us)
Async XLA Ops:
  7.2 1.0 copy-start
  7.2 104.8 %all-gather.3.cloned.1.call-start = ((), (), s32[]{:S(2)}) async-start(), calls=%async_computation.2 | async-start | bytes 8650752 | tf_op jit(solution)/shard_map/all_gather | solution.py:25
  10.0 147.5 %reduce-scatter.3.cloned.1.call-start = ((), (), s32[]{:S(2)}) async-start(), calls=%async_computation.3 | async-start | bytes 2359296 | tf_op jit(solution)/shard_map/reduce_scatter | solution.py:43
  112.0 9.5 %copy-start.2 = (bf16[1,1,96,128,128]{4,3,2,1,0:T(8,128)(2,1)S(1)}, bf16[1,1,96,128,128]{4,3,2,1,0:T(8,128)(2,1)}, u32[]{:S(2)}) copy-start(bf16[1,1,96,128,128]{4,3,2,1,0:T(8,128)(2,1)} %param.16) | copy-start | bytes 9437188
  121.5 36.0 %copy-start.5 = (bf16[256,256]{1,0:T(8,128)(2,1)S(1)}, bf16[256,256]{1,0:T(8,128)(2,1)}, u32[]{:S(2)}) copy-start(bf16[256,256]{1,0:T(8,128)(2,1)} %param.11) | copy-start | bytes 393220
  127.0 61.6 %all-gather.5.cloned.1.call-start = ((), (), s32[]{:S(2)}) async-start(), calls=%async_computation.4 | async-start | bytes 2359296 | tf_op jit(solution)/shard_map/all_gather | solution.py:48
  159.8 328.4 %reduce-scatter.5.cloned.1.call-start = ((), (), s32[]{:S(2)}) async-start(), calls=%async_computation.5 | async-start | bytes 8650752 | tf_op jit(solution)/shard_map/reduce_scatter | solution.py:62
  209.2 7.9 %copy-start.6 = (s32[1,1,96]{2,1,0:T(1,128)S(1)}, s32[1,1,96]{2,1,0:T(1,128)}, u32[]{:S(2)}) copy-start(s32[1,1,96]{2,1,0:T(1,128)} %param.14) | copy-start | bytes 1156
  255.1 78.7 %copy-start.3 = (bf16[512,256]{1,0:T(8,128)(2,1)S(1)}, bf16[512,256]{1,0:T(8,128)(2,1)}, u32[]{:S(2)}) copy-start(bf16[512,256]{1,0:T(8,128)(2,1)} %get-tuple-element.21) | copy-start | bytes 786436
  255.1 79.7 %copy-start.1 = (bf16[4096,256]{1,0:T(8,128)(2,1)S(1)}, bf16[4096,256]{1,0:T(8,128)(2,1)}, u32[]{:S(2)}) copy-start(bf16[4096,256]{1,0:T(8,128)(2,1)} %all-gather.5.cloned.1.call-done) | copy-start | bytes 6291460
  255.2 493.4 %all-reduce.3.cloned.1.call-start = ((), (), s32[]{:S(2)}) async-start(), calls=%async_computation.6 | async-start | bytes 1048576 | tf_op jit(solution)/shard_map/psum | solution.py:73
  348.7 141.5 %copy-start.4 = (bf16[256,256]{1,0:T(8,128)(2,1)S(1)}, bf16[256,256]{1,0:T(8,128)(2,1)}, u32[]{:S(2)}) copy-start(bf16[256,256]{1,0:T(8,128)(2,1)} %param.10) | copy-start | bytes 393220
Sparse Core Ops, SparseCore 0:
  11.1 100.8 all-gather.2
  127.1 30.3 reduce-scatter.2
  159.9 28.6 all-gather.4
  255.3 232.8 reduce-scatter.4
  494.2 254.3 all-reduce.2
where the time goes:
time: 758 us
  waiting for transfers between devices  550 us (73%)
  blocking collectives  78.1 us (10%)
  other arithmetic  46.2 us (6%)
  local copies, waits for them, and re-layouts  38.4 us (5%)
  matrix products  30 us (4%)
  between operations  14.5 us (2%)
    psum x1, waiting for transfers between devices, per_device(): lax.psum((local_msg, local_self, local_bias), ('row', 'col'))  256 us
    reduce_scatter x1, waiting for transfers between devices, per_device(): lax.psum_scatter(back_part.astype(jnp.bfloat16), 'row', scatter_dimension...  134 us
    all_gather x1, waiting for transfers between devices, per_device(): column_msgs = lax.all_gather(messages, 'row', axis=0, tiled=True)  101 us
    psum x1, blocking collectives, per_device(): lax.psum((local_msg, local_self, local_bias), ('row', 'col'))  78.1 us
    reduce_scatter x1, waiting for transfers between devices, per_device(): lax.psum_scatter(partial_value.astype(jnp.bfloat16), 'col', scatter_dimen...  30.4 us
    scatter-add x1, other arithmetic, per_device(): jax.ops.segment_sum(backward, slot_cols, num_segments=tile_cols)  29.1 us
    all_gather x1, waiting for transfers between devices, per_device(): grad_rows_all = lax.all_gather(grad_pre, 'col', axis=0, tiled=True)  28.7 us
  transfers between devices with their start and end apart: 5, of which 5 were waited for; matrix products, arithmetic and copies ran while one was open for 3% of the time, Pallas kernels for 0%

commit v1 on v0

--- a/solution.py
+++ b/solution.py
@@ -3,6 +3,11 @@
 import jax.numpy as jnp
 from jax import lax
 from jax.sharding import PartitionSpec as P
+
+
+def axis_by_axis(value, first, second):
+    half = lax.psum(value, first)
+    return lax.psum(half, second)
 
 
 def activate(pre, row_mask, grad_in):
@@ -70,8 +75,8 @@
     local_msg = jnp.einsum("hf,hg->fg", feats, grad_msg, preferred_element_type=jnp.float32)
     local_self = jnp.einsum("hf,hg->fg", feats, grad_pre, preferred_element_type=jnp.float32)
     local_bias = jnp.sum(grad_pre.astype(jnp.float32), axis=0)
-    total_msg, total_self, total_bias = lax.psum(
-        (local_msg, local_self, local_bias), ("row", "col")
+    total_msg, total_self, total_bias = axis_by_axis(
+        (local_msg, local_self, local_bias), "col", "row"
     )
     factor = 1.0 / math.sqrt(own_rows * row_count * col_count)
     return (

time: 758 us -> 717 us (0.946)
  waiting for transfers between devices: 550 us -> 501 us
  blocking collectives: 78.1 us -> 87 us
    psum x1 -> x2, waiting for transfers between devices: 256 us -> 197 us  [the longest x1 147 us: axis_by_axis(): return lax.psum(half, second)]
    reduce_scatter x1, waiting for transfers between devices: 134 us -> 144 us  [per_device(): lax.psum_scatter(back_part.astype(jnp.bfloat16), 'row', scatter_dimension...]
    psum x1 -> x2, blocking collectives: 78.1 us -> 87 us  [the longest x1 75 us: axis_by_axis(): return lax.psum(half, second)]
  transfers between devices with their start and end apart: 5 -> 6, of which waited for: 5 -> 6; matrix products, arithmetic and copies ran while one was open for 3% -> 3% of each run, Pallas kernels for 0% -> 0%
where the time goes in v1:
time: 717 us; the launch traced here: 716 us
  waiting for transfers between devices  501 us (70%)
  blocking collectives  87 us (12%)
  other arithmetic  46.2 us (6%)
  local copies, waits for them, and re-layouts  38.4 us (5%)
  matrix products  29 us (4%)
  between operations  14.8 us (2%)
    psum x1, waiting for transfers between devices, axis_by_axis(): return lax.psum(half, second)  147 us
    reduce_scatter x1, waiting for transfers between devices, per_device(): lax.psum_scatter(back_part.astype(jnp.bfloat16), 'row', scatter_dimension...  144 us
    all_gather x1, waiting for transfers between devices, per_device(): column_msgs = lax.all_gather(messages, 'row', axis=0, tiled=True)  101 us
    psum x1, blocking collectives, axis_by_axis(): return lax.psum(half, second)  75 us
    psum x1, waiting for transfers between devices, axis_by_axis(): half = lax.psum(value, first)  49.3 us
    reduce_scatter x1, waiting for transfers between devices, per_device(): lax.psum_scatter(partial_value.astype(jnp.bfloat16), 'col', scatter_dimen...  30.4 us
    scatter-add x1, other arithmetic, per_device(): jax.ops.segment_sum(backward, slot_cols, num_segments=tile_cols)  29.1 us
    all_gather x1, waiting for transfers between devices, per_device(): grad_rows_all = lax.all_gather(grad_pre, 'col', axis=0, tiled=True)  28.7 us
  transfers between devices with their start and end apart: 6, of which 6 were waited for; matrix products, arithmetic and copies ran while one was open for 3% of the time, Pallas kernels for 0%

profile of v1, /device:TPU:2, one launch (start us, length us, event | category | flops | bytes accessed | tf_op | source)
XLA Modules:
  0.0 716.3 jit_solution(9305779169490277103)
XLA Ops:
  7.2 0.0 copy-start
  7.2 0.0 all-gather.3.cloned.1.call-start
  7.2 0.7 convert_element_type.67
  7.9 0.2 copy-done
  8.1 1.8 fusion.12
  10.0 0.0 all-gather.3.cloned.1.call-update
  10.0 0.0 reduce-scatter.3.cloned.1.call-start
  10.7 0.7 fusion.16
  11.4 100.7 %all-gather.3.cloned.1.call-done = bf16[16384,256]{1,0:T(8,128)(2,1)} async-done(((bf16[512,256]{1,0:T(8,128)(2,1)}), bf16[16384,256]{1,0:T(8,128)(2,1)}) %all-gather.3.cloned.1.call-update) | async-done | bytes 8388624 | tf_op jit(solution)/shard_map/all_gather | solution.py:30
  112.0 9.5 %gather_fusion = bf16[96,128,256]{2,1,0:T(8,128)(2,1)} fusion(bf16[128,128,256]{2,1,0:T(8,128)(2,1)} %bitcast.53, s32[1024]{0:T(1024)S(1)} %pad_clamp_fusion), kind=kCustom, calls=%fused_computation | custom fusion | bytes 12583296 | tf_op jit(solution)/shard_map/gather | solution.py:42
  121.5 0.0 copy-done.2
  121.5 5.5 bitcast_convert_fusion
  127.0 0.0 reduce-scatter.3.cloned.1.call-update
  127.0 0.0 all-gather.5.cloned.1.call-start
  127.1 30.4 %reduce-scatter.3.cloned.1.call-done = bf16[512,256]{1,0:T(8,128)(2,1)} async-done(((bf16[4096,256]{1,0:T(8,128)(2,1)}), bf16[512,256]{1,0:T(8,128)(2,1)}) %reduce-scatter.3.cloned.1.call-update) | async-done | bytes 262160 | tf_op jit(solution)/shard_map/reduce_scatter | solution.py:48
  157.5 0.0 copy-done.6
  157.5 2.3 convert_reduce_fusion
  159.8 0.0 all-gather.5.cloned.1.call-update
  159.8 0.0 reduce-scatter.5.cloned.1.call-start
  159.9 28.7 %all-gather.5.cloned.1.call-done = bf16[4096,256]{1,0:T(8,128)(2,1)} async-done(((bf16[512,256]{1,0:T(8,128)(2,1)}), bf16[4096,256]{1,0:T(8,128)(2,1)}) %all-gather.5.cloned.1.call-update) | async-done | bytes 2097168 | tf_op jit(solution)/shard_map/all_gather | solution.py:53
  188.6 8.0 %convolution_bitcast_fusion = f32[3,32,128,256]{2,3,0,1:T(8,128)} fusion(bf16[32,128,256,1]{2,1,3,0:T(8,128)(2,1)} %bitcast.51, bf16[3,32,128,128]{3,2,1,0:T(8,128)(2,1)S(1)} %bitcast.55, bf16[3,32]{0,1:T(8,128)(2,1)S(1)} %fusion.15), kind=kOutput, calls=%fused_computation.7 | convolution fusion | flops 811597824 | bytes 17825984 | tf_op jit(solution)/shard_map/krij,rif->krjf/dot_general | solution.py:55
  196.6 12.6 %copy.22 = f32[3,32,128,256]{3,2,1,0:T(8,128)} copy(f32[3,32,128,256]{2,3,0,1:T(8,128)} %convolution_bitcast_fusion) | data formatting | bytes 25165824 | tf_op jit(solution)/shard_map/krij,rif->krjf/transpose | solution.py:55
  209.2 7.8 %broadcast_in_dim.2 = f32[128,128,256]{2,1,0:T(8,128)} broadcast(f32[]{:T(128)} %constant.4.clone.1), dimensions={} | broadcast | bytes 16777220 | tf_op jit(solution)/shard_map/broadcast_in_dim | solution.py:58
  217.0 0.0 copy-done.7
  217.0 29.1 %scatter_fusion = f32[128,128,256]{2,1,0:T(8,128)} fusion(f32[128,128,256]{2,1,0:T(8,128)} %broadcast_in_dim.2, s32[96]{0:T(128)S(1)} %bitcast.57, f32[96,128,256]{2,1,0:T(8,128)} %bitcast.46), kind=kCustom, calls=%fused_computation.1 | custom fusion | flops 3145728 | bytes 37749120 | tf_op jit(solution)/shard_map/scatter-add | solution.py:58
  246.1 9.0 %convert_element_type.75 = bf16[128,128,256]{2,1,0:T(8,128)(2,1)} convert(f32[128,128,256]{2,1,0:T(8,128)} %scatter_fusion) | non-fusion elementwise | flops 4194304 | bytes 25165824 | tf_op jit(solution)/shard_map/convert_element_type | solution.py:68
  255.1 0.0 reduce-scatter.5.cloned.1.call-update
  255.2 0.0 all-reduce.7.cloned.1.call-start
  255.2 12.0 %psum.46 = f32[256]{0:T(256)S(1)} all-reduce(f32[256]{0:T(256)S(1)} %get-tuple-element.22), channel_id=1, replica_groups=mesh['row'=32,'col'=8] {'col'}, use_global_device_ids=true, to_apply=%region_8.0 | all-reduce | flops 256 | bytes 2048 | tf_op jit(solution)/shard_map/psum | solution.py:9
  267.2 75.0 %psum.47 = f32[256]{0:T(256)S(1)} all-reduce(f32[256]{0:T(256)S(1)} %psum.46), channel_id=1, replica_groups=mesh['row'=32,'col'=8] {'row'}, use_global_device_ids=true, to_apply=%region_9.0 | all-reduce | flops 256 | bytes 2048 | tf_op jit(solution)/shard_map/psum | solution.py:10
  342.2 0.6 broadcast_multiply_fusion.2
  342.8 1.0 convolution_bitcast_fusion.1
  343.8 144.1 %reduce-scatter.5.cloned.1.call-done = bf16[512,256]{1,0:T(8,128)(2,1)} async-done(((bf16[16384,256]{1,0:T(8,128)(2,1)}), bf16[512,256]{1,0:T(8,128)(2,1)}) %reduce-scatter.5.cloned.1.call-update) | async-done | bytes 262160 | tf_op jit(solution)/shard_map/reduce_scatter | solution.py:67
  487.8 2.0 convolution_bitcast_fusion.2
  489.8 0.0 all-reduce.7.cloned.1.call-update
  489.9 0.2 all-reduce.5.cloned.1.call-start
  490.1 0.0 copy-done.1
  490.1 7.2 %fusion.4 = f32[3,32,128,128]{2,3,0,1:T(8,128)} fusion(bf16[32,128,256,1]{2,1,3,0:T(8,128)(2,1)S(1)} %bitcast.52, bf16[3,32,128,256]{3,2,1,0:T(8,128)(2,1)} %bitcast.49), kind=kOutput, calls=%fused_computation.10 | convolution fusion | flops 805306368 | bytes 14680064 | tf_op jit(solution)/shard_map/rif,krjf->krij/dot_general | solution.py:62
  497.3 6.5 copy.24
  503.9 49.3 %all-reduce.7.cloned.1.call-done = (f32[256,256]{0,1:T(8,128)}, f32[256,256]{0,1:T(8,128)}) async-done(((f32[256,256]{0,1:T(8,128)}, f32[256,256]{0,1:T(8,128)}), (f32[256,256]{0,1:T(8,128)}, f32[256,256]{0,1:T(8,128)})) %all-reduce.7.cloned.1.call-update) | async-done | bytes 524304 | tf_op jit(solution)/shard_map/psum | solution.py:9
  553.1 0.0 all-reduce.5.cloned.1.call-update
  553.1 5.0 multiply_convert_fusion
  558.2 0.3 fusion.14
  558.4 1.0 fusion.13
  559.4 147.3 %all-reduce.5.cloned.1.call-done = (f32[256,256]{0,1:T(8,128)}, f32[256,256]{0,1:T(8,128)}) async-done(((f32[256,256]{0,1:T(8,128)}, f32[256,256]{0,1:T(8,128)}), (f32[256,256]{0,1:T(8,128)}, f32[256,256]{0,1:T(8,128)})) %all-reduce.5.cloned.1.call-update) | async-done | bytes 524304 | tf_op jit(solution)/shard_map/psum | solution.py:10
  706.7 1.1 broadcast_multiply_fusion
  707.8 0.8 copy.26
  708.6 0.8 copy.25
  (13 shorter events, 0.0 us)
Async XLA Ops:
  7.2 1.0 copy-start
  7.2 104.8 %all-gather.3.cloned.1.call-start = ((), (), s32[]{:S(2)}) async-start(), calls=%async_computation.2 | async-start | bytes 8650752 | tf_op jit(solution)/shard_map/all_gather | solution.py:30
  10.0 147.5 %reduce-scatter.3.cloned.1.call-start = ((), (), s32[]{:S(2)}) async-start(), calls=%async_computation.3 | async-start | bytes 2359296 | tf_op jit(solution)/shard_map/reduce_scatter | solution.py:48
  112.0 9.5 %copy-start.2 = (bf16[1,1,96,128,128]{4,3,2,1,0:T(8,128)(2,1)S(1)}, bf16[1,1,96,128,128]{4,3,2,1,0:T(8,128)(2,1)}, u32[]{:S(2)}) copy-start(bf16[1,1,96,128,128]{4,3,2,1,0:T(8,128)(2,1)} %param.16) | copy-start | bytes 9437188
  121.5 36.0 %copy-start.6 = (bf16[256,256]{1,0:T(8,128)(2,1)S(1)}, bf16[256,256]{1,0:T(8,128)(2,1)}, u32[]{:S(2)}) copy-start(bf16[256,256]{1,0:T(8,128)(2,1)} %param.11) | copy-start | bytes 393220
  127.0 61.6 %all-gather.5.cloned.1.call-start = ((), (), s32[]{:S(2)}) async-start(), calls=%async_computation.4 | async-start | bytes 2359296 | tf_op jit(solution)/shard_map/all_gather | solution.py:53
  159.8 328.0 %reduce-scatter.5.cloned.1.call-start = ((), (), s32[]{:S(2)}) async-start(), calls=%async_computation.5 | async-start | bytes 8650752 | tf_op jit(solution)/shard_map/reduce_scatter | solution.py:67
  209.2 7.9 %copy-start.7 = (s32[1,1,96]{2,1,0:T(1,128)S(1)}, s32[1,1,96]{2,1,0:T(1,128)}, u32[]{:S(2)}) copy-start(s32[1,1,96]{2,1,0:T(1,128)} %param.14) | copy-start | bytes 1156
  255.1 87.6 %copy-start.3 = (bf16[512,256]{1,0:T(8,128)(2,1)S(1)}, bf16[512,256]{1,0:T(8,128)(2,1)}, u32[]{:S(2)}) copy-start(bf16[512,256]{1,0:T(8,128)(2,1)} %get-tuple-element.23) | copy-start | bytes 786436
  255.1 235.0 %copy-start.1 = (bf16[4096,256]{1,0:T(8,128)(2,1)S(1)}, bf16[4096,256]{1,0:T(8,128)(2,1)}, u32[]{:S(2)}) copy-start(bf16[4096,256]{1,0:T(8,128)(2,1)} %all-gather.5.cloned.1.call-done) | copy-start | bytes 6291460
  255.2 297.9 %all-reduce.7.cloned.1.call-start = ((), (), s32[]{:S(2)}) async-start(), calls=%async_computation.7 | async-start | bytes 1048576 | tf_op jit(solution)/shard_map/psum | solution.py:9
  489.9 216.8 %all-reduce.5.cloned.1.call-start = ((), (), s32[]{:S(2)}) async-start(), calls=%async_computation.6 | async-start | bytes 1048576 | tf_op jit(solution)/shard_map/psum | solution.py:10
  503.8 54.3 %copy-start.4 = (bf16[512,256]{1,0:T(8,128)(2,1)S(1)}, bf16[512,256]{1,0:T(8,128)(2,1)}, u32[]{:S(2)}) copy-start(bf16[512,256]{1,0:T(8,128)(2,1)} %reduce-scatter.5.cloned.1.call-done) | copy-start | bytes 786436
  503.8 54.3 %copy-start.5 = (bf16[256,256]{1,0:T(8,128)(2,1)S(1)}, bf16[256,256]{1,0:T(8,128)(2,1)}, u32[]{:S(2)}) copy-start(bf16[256,256]{1,0:T(8,128)(2,1)} %param.10) | copy-start | bytes 393220
Sparse Core Ops, SparseCore 0:
  11.1 100.8 all-gather.2
  127.1 30.3 reduce-scatter.2
  159.9 28.6 all-gather.4
  255.3 232.4 reduce-scatter.4
  490.7 62.4 all-reduce.6
  556.4 150.2 all-reduce.4
